TPU v7x, 32 devices: a whole 2x2x4 slice. The times are simulated.
32 devices in a mesh: gx: 8 (over z, y), gy: 4 (over x, core).
Axes of the slice: x: 2, y: 2, z: 4, core: 2. Of those that a mesh axis runs over, the one named last changes fastest.
Arguments:
- cotangent: float32 [2, 128, 1536], P(None, 'gx', 'gy'), may hold values from -12 to 12
- velocity_in: bfloat16 [2, 128, 1536], P(None, 'gx', 'gy'), may hold values from -6 to 6
- hidden_pre1: bfloat16 [64, 128, 1536], P(None, 'gx', 'gy'), may hold values from -6 to 6
- hidden_pre2: bfloat16 [64, 128, 1536], P(None, 'gx', 'gy'), may hold values from -6 to 6
- w_first: bfloat16 [9, 64, 2], replicated, may hold values from -1.5 to 1.5
- w_middle: bfloat16 [9, 64, 64], replicated, may hold values from -0.25 to 0.25
- w_last: bfloat16 [9, 2, 64], replicated, may hold values from -0.25 to 0.25
Outputs:
- grad_velocity: float32 [2, 128, 1536], P(None, 'gx', 'gy')
- grad_first: float32 [9, 64, 2], replicated
- grad_middle: float32 [9, 64, 64], replicated
- grad_last: float32 [9, 2, 64], replicated
- grad_bias1: float32 [64], replicated
- grad_bias2: float32 [64], replicated
All inputs are finite; a program needn't handle non-finite values.
Results may differ from a plain program's by a relative error of at most 0.0075.
Values may be sent and summed in bfloat16 or wider, within the bound.
A program may use at most 64 MiB of HBM per device.

v0:
```python
import math
import jax
import jax.numpy as jnp
from jax import lax
from jax.sharding import PartitionSpec as P

ITERS = 4
OFFSETS = ((-1, -1), (-1, 0), (-1, 1), (0, -1), (0, 0), (0, 1), (1, -1), (1, 0), (1, 1))


def with_halo(shard, sides, width):
    for axis, dim in sides:
        count, length = (lax.axis_size(axis), shard.shape[dim])
        up = [(i, (i + 1) % count) for i in range(count)]
        down = [(j, i) for i, j in up]
        last = lax.slice_in_dim(shard, length - width, length, axis=dim)
        leading = lax.slice_in_dim(shard, 0, width, axis=dim)
        before = lax.ppermute(last, axis, up)
        after = lax.ppermute(leading, axis, down)
        shard = jnp.concatenate([before, shard, after], axis=dim)
    return shard


def gelu_slope(pre):
    values = pre.astype(jnp.float32)
    _, pullback = jax.vjp(lambda inner: jax.nn.gelu(inner, approximate=True), values)
    return pullback(jnp.ones_like(values))[0]


def window(padded, row_step, col_step, rows, cols):
    return padded[:, 1 + row_step : 1 + row_step + rows, 1 + col_step : 1 + col_step + cols]


def channel_border(field):
    return with_halo(field, (("gx", 1), ("gy", 2)), 1)


def stencil_apply(field):
    padded = with_halo(field, (("gx", 0), ("gy", 1)), 2)
    beside = padded[:-4, 2:-2] + padded[4:, 2:-2] + padded[2:-2, :-4]
    beside = beside + padded[2:-2, 4:]
    return (padded, field - 0.25 * beside)


def paired_sums(residual, image):
    return lax.psum((jnp.sum(residual * residual), jnp.sum(residual * image)), ("gx", "gy"))


def conv_back(weights, padded, rows, cols):
    channels = padded.shape[0]
    total = jnp.zeros((weights.shape[2], rows * cols), jnp.float32)
    for index, (row_step, col_step) in enumerate(OFFSETS):
        shifted = window(padded, -row_step, -col_step, rows, cols).reshape(channels, -1)
        total = total + lax.dot_general(
            weights[index], shifted, (((0,), (0,)), ((), ())), preferred_element_type=jnp.float32
        )
    return total.reshape(weights.shape[2], rows, cols)


def grads_from_padded_deltas(delta_pad, inputs, rows, cols):
    flat_inputs = inputs.reshape(inputs.shape[0], -1)
    results = []
    for row_step, col_step in OFFSETS:
        shifted = window(delta_pad, -row_step, -col_step, rows, cols).reshape(
            delta_pad.shape[0], -1
        )
        results.append(
            lax.dot_general(
                shifted, flat_inputs, (((1,), (1,)), ((), ())), preferred_element_type=jnp.float32
            )
        )
    return jnp.stack(results)


def per_device(cotangent, velocity_in, hidden_pre1, hidden_pre2, w_first, w_middle, w_last):
    rows = cotangent.shape[1]
    cols = cotangent.shape[2]
    factor = 1.0 / math.sqrt(rows * lax.axis_size("gx") * cols * lax.axis_size("gy"))
    hidden1 = jax.nn.gelu(hidden_pre1.astype(jnp.float32), approximate=True).astype(jnp.bfloat16)
    hidden2 = jax.nn.gelu(hidden_pre2.astype(jnp.float32), approximate=True).astype(jnp.bfloat16)
    slope1 = gelu_slope(hidden_pre1)
    slope2 = gelu_slope(hidden_pre2)
    cot_pad = with_halo(cotangent, (("gx", 1), ("gy", 2)), 1)
    along_rows = cot_pad[0, 2:, 1:-1] - cot_pad[0, :-2, 1:-1]
    along_cols = cot_pad[1, 1:-1, 2:] - cot_pad[1, 1:-1, :-2]
    rhs = -0.5 * (along_rows + along_cols)
    lam_pad = jnp.zeros((rows + 4, cols + 4), jnp.float32)
    residual = rhs
    resid_pad, image = stencil_apply(residual)
    norm_now, product = paired_sums(residual, image)
    alpha = norm_now / product
    dir_pad = resid_pad
    along = image
    for step in range(ITERS):
        lam_pad = lam_pad + alpha * dir_pad
        if step + 1 < ITERS:
            residual = residual - alpha * along
            resid_pad, image = stencil_apply(residual)
            norm_next, product = paired_sums(residual, image)
            ratio = norm_next / norm_now
            alpha = norm_next / (product - ratio * norm_next / alpha)
            dir_pad = resid_pad + ratio * dir_pad
            along = image + ratio * along
            norm_now = norm_next
    adjoint_rows = 0.5 * (lam_pad[0 : rows + 2, 1 : cols + 3] - lam_pad[2 : rows + 4, 1 : cols + 3])
    adjoint_cols = 0.5 * (lam_pad[1 : rows + 3, 0 : cols + 2] - lam_pad[1 : rows + 3, 2 : cols + 4])
    adjoint_pad = cot_pad + jnp.stack([adjoint_rows, adjoint_cols])
    adjoint_b = adjoint_pad.astype(jnp.bfloat16)
    delta2 = (conv_back(w_last, adjoint_b, rows, cols) * slope2).astype(jnp.bfloat16)
    delta2_pad = channel_border(delta2)
    delta1 = (conv_back(w_middle, delta2_pad, rows, cols) * slope1).astype(jnp.bfloat16)
    grad_last = grads_from_padded_deltas(adjoint_b, hidden2, rows, cols)
    grad_middle = grads_from_padded_deltas(delta2_pad, hidden1, rows, cols)
    delta1_pad = channel_border(delta1)
    spread = conv_back(w_first, delta1_pad, rows, cols)
    grad_first = grads_from_padded_deltas(delta1_pad, velocity_in, rows, cols)
    grad_velocity = adjoint_pad[:, 1:-1, 1:-1] + spread
    bias_one = jnp.sum(delta1.astype(jnp.float32), axis=(1, 2))
    bias_two = jnp.sum(delta2.astype(jnp.float32), axis=(1, 2))
    summed = lax.psum((grad_first, grad_middle, grad_last, bias_one, bias_two), ("gx", "gy"))
    return (
        grad_velocity,
        factor * summed[0],
        factor * summed[1],
        factor * summed[2],
        factor * summed[3],
        factor * summed[4],
    )


def solution(mesh):
    return jax.shard_map(
        per_device,
        mesh=mesh,
        in_specs=(
            P(None, "gx", "gy"),
            P(None, "gx", "gy"),
            P(None, "gx", "gy"),
            P(None, "gx", "gy"),
            P(),
            P(),
            P(),
        ),
        out_specs=(P(None, "gx", "gy"), P(), P(), P(), P(), P()),
        check_vma=False,
    )
```

profile of v0, /device:TPU:8, one launch (start us, length us, event | category | flops | bytes accessed | tf_op | source)
XLA Modules:
  0.0 423.0 jit_solution(12630795308313707400)
XLA Ops:
  10.9 1.6 collective-permute-done
  15.5 2.0 collective-permute-done.2
  18.5 2.5 collective-permute-start.4
  24.6 1.7 collective-permute-start.7
  28.4 42.3 %all-reduce.4 = (f32[]{:T(128)}, f32[]{:T(128)}) all-reduce(f32[]{:T(128)} %get-tuple-element.25, f32[]{:T(128)} %get-tuple-element.24), channel_id=1, replica_groups=mesh['gx'=8,'gy'=4] {'gx','gy'}, use_global_device_ids=true, to_apply=%region_1.0 | all-reduce | flops 2 | bytes 16 | tf_op jit(solution)/shard_map/psum | solution.py:46
  72.1 2.5 collective-permute-start.8
  78.3 1.7 collective-permute-start.11
  82.1 41.4 %all-reduce.3 = (f32[]{:T(128)}, f32[]{:T(128)}) all-reduce(f32[]{:T(128)} %get-tuple-element.23, f32[]{:T(128)} %get-tuple-element.22), channel_id=1, replica_groups=mesh['gx'=8,'gy'=4] {'gx','gy'}, use_global_device_ids=true, to_apply=%region_5.0 | all-reduce | flops 2 | bytes 16 | tf_op jit(solution)/shard_map/psum | solution.py:46
  128.3 2.5 collective-permute-start.12
  134.4 1.7 collective-permute-start.15
  138.3 41.7 %all-reduce.2 = (f32[]{:T(128)}, f32[]{:T(128)}) all-reduce(f32[]{:T(128)} %get-tuple-element.21, f32[]{:T(128)} %get-tuple-element.20), channel_id=1, replica_groups=mesh['gx'=8,'gy'=4] {'gx','gy'}, use_global_device_ids=true, to_apply=%region_9.0 | all-reduce | flops 2 | bytes 16 | tf_op jit(solution)/shard_map/psum | solution.py:46
  184.1 2.5 collective-permute-start.16
  190.3 1.7 collective-permute-start.19
  194.1 41.4 %all-reduce.1 = (f32[]{:T(128)}, f32[]{:T(128)}) all-reduce(f32[]{:T(128)} %get-tuple-element.19, f32[]{:T(128)} %get-tuple-element.18), channel_id=1, replica_groups=mesh['gx'=8,'gy'=4] {'gx','gy'}, use_global_device_ids=true, to_apply=%region_13.0 | all-reduce | flops 2 | bytes 16 | tf_op jit(solution)/shard_map/psum | solution.py:46
  249.2 2.5 collective-permute-start.20
  252.6 1.6 collective-permute-done.20
  256.0 1.7 collective-permute-start.22
  258.1 5.7 %collective-permute-done.23 = bf16[64,18,1]{2,0,1:T(8,128)(2,1)S(1)} collective-permute-done((bf16[64,18,1]{2,0,1:T(8,128)(2,1)S(1)}, bf16[64,18,1]{2,0,1:T(8,128)(2,1)S(1)}, u32[]{:S(2)}, u32[]{:S(2)}) %collective-permute-start.23) | collective-permute-done | bytes 2336 | tf_op jit(solution)/shard_map/ppermute | solution.py:18
  278.6 2.7 collective-permute-start.24
  289.5 2.7 collective-permute-done.27
  292.2 2.7 collective-permute-done.26
  301.3 43.5 %all-reduce = (f32[9,64,2]{1,2,0:T(2,128)S(1)}, f32[9,2,64]{2,1,0:T(2,128)S(1)}, f32[64]{0:T(128)S(1)}, f32[64]{0:T(128)S(1)}) all-reduce(f32[9,64,2]{1,2,0:T(2,128)S(1)} %fusion.40, f32[9,2,64]{2,1,0:T(2,128)S(1)} %fusion.31, f32[64]{0:T(128)S(1)} %get-tuple-element.40, ...), channel_id=1, replica_groups=mesh['gx'=8,'gy'=4] {'gx','gy'}, use_global_device_ids=true, to_apply=%region_16.0 | all-reduce | flops 2432 | bytes 19456 | tf_op jit(solution)/shard_map/psum | solution.py:120
  352.6 61.8 %all-reduce.7.cloned.1.call-done = f32[9,64,64]{2,1,0:T(8,128)} async-done(((f32[9,64,64]{2,1,0:T(8,128)}), f32[9,64,64]{2,1,0:T(8,128)}) %all-reduce.7.cloned.1.call-update) | async-done | bytes 147472 | tf_op jit(solution)/shard_map/psum | solution.py:120
  414.4 1.7 broadcast_multiply_fusion
  (181 shorter events, 80.4 us)
Async XLA Ops:
  7.2 407.2 %all-reduce.7.cloned.1.call-start = ((), (), s32[]{:S(2)}) async-start(), calls=%async_computation | async-start | bytes 589824 | tf_op jit(solution)/shard_map/psum | solution.py:120
  8.0 4.5 %collective-permute-start = (f32[2,1,384]{2,1,0:T(1,128)S(1)}, f32[2,1,384]{2,1,0:T(1,128)S(1)}, u32[]{:S(2)}, u32[]{:S(2)}) collective-permute-start(f32[2,1,384]{2,1,0:T(1,128)S(1)} %get-tuple-element.78), channel_id=1, source_target_pairs={{0,4},{4,8},{8,12},{12,16},{16,20},{20,24},{24,28},{28,0},{1,5},{5... | collective-permute-start | bytes 9224 | tf_op jit(solution)/shard_map/ppermute | solution.py:18
  9.5 3.6 collective-permute-start.1
  14.0 3.5 collective-permute-start.2
  18.5 4.5 %collective-permute-start.4 = (f32[2,384]{1,0:T(2,128)S(1)}, f32[2,384]{1,0:T(2,128)S(1)}, u32[]{:S(2)}, u32[]{:S(2)}) collective-permute-start(f32[2,384]{1,0:T(2,128)S(1)} %get-tuple-element.103), channel_id=1, source_target_pairs={{0,4},{4,8},{8,12},{12,16},{16,20},{20,24},{24,28},{28,0},{1,5},{5... | collective-permute-start | bytes 9224 | tf_op jit(solution)/shard_map/ppermute | solution.py:18
  20.9 3.6 collective-permute-start.5
  24.6 3.1 collective-permute-start.7
  72.1 4.5 %collective-permute-start.8 = (f32[2,384]{1,0:T(2,128)S(1)}, f32[2,384]{1,0:T(2,128)S(1)}, u32[]{:S(2)}, u32[]{:S(2)}) collective-permute-start(f32[2,384]{1,0:T(2,128)S(1)} %get-tuple-element.101), channel_id=1, source_target_pairs={{0,4},{4,8},{8,12},{12,16},{16,20},{20,24},{24,28},{28,0},{1,5},{5... | collective-permute-start | bytes 9224 | tf_op jit(solution)/shard_map/ppermute | solution.py:18
  74.6 3.6 collective-permute-start.9
  78.3 3.1 collective-permute-start.11
  128.3 4.5 %collective-permute-start.12 = (f32[2,384]{1,0:T(2,128)S(1)}, f32[2,384]{1,0:T(2,128)S(1)}, u32[]{:S(2)}, u32[]{:S(2)}) collective-permute-start(f32[2,384]{1,0:T(2,128)S(1)} %get-tuple-element.99), channel_id=1, source_target_pairs={{0,4},{4,8},{8,12},{12,16},{16,20},{20,24},{24,28},{28,0},{1,5},{5... | collective-permute-start | bytes 9224 | tf_op jit(solution)/shard_map/ppermute | solution.py:18
  130.8 3.6 collective-permute-start.13
  134.4 3.1 collective-permute-start.15
  184.1 4.5 %collective-permute-start.16 = (f32[2,384]{1,0:T(2,128)S(1)}, f32[2,384]{1,0:T(2,128)S(1)}, u32[]{:S(2)}, u32[]{:S(2)}) collective-permute-start(f32[2,384]{1,0:T(2,128)S(1)} %get-tuple-element.97), channel_id=1, source_target_pairs={{0,4},{4,8},{8,12},{12,16},{16,20},{20,24},{24,28},{28,0},{1,5},{5... | collective-permute-start | bytes 9224 | tf_op jit(solution)/shard_map/ppermute | solution.py:18
  186.6 3.6 collective-permute-start.17
  190.3 3.1 collective-permute-start.19
  249.2 5.0 %collective-permute-start.20 = (bf16[64,1,384]{2,0,1:T(8,128)(2,1)S(1)}, bf16[64,1,384]{2,0,1:T(8,128)(2,1)S(1)}, u32[]{:S(2)}, u32[]{:S(2)}) collective-permute-start(bf16[64,1,384]{2,0,1:T(8,128)(2,1)S(1)} %get-tuple-element.72), channel_id=1, source_target_pairs={{0,4},{4,8},{8,12},{12,16},{16,20},{20,24},{24,28},{28,0},{1,5},{5... | collective-permute-start | bytes 147464 | tf_op jit(solution)/shard_map/ppermute | solution.py:18
  251.7 4.1 collective-permute-start.21
  256.0 7.8 %collective-permute-start.23 = (bf16[64,18,1]{2,0,1:T(8,128)(2,1)S(1)}, bf16[64,18,1]{2,0,1:T(8,128)(2,1)S(1)}, u32[]{:S(2)}, u32[]{:S(2)}) collective-permute-start(bf16[64,18,1]{2,0,1:T(8,128)(2,1)S(1)} %get-tuple-element.63), channel_id=1, source_target_pairs={{0,1},{1,2},{2,3},{3,0},{4,5},{5,6},{6,7},{7,4},{8,9},{9,10},{10,1... | collective-permute-start | bytes 6920 | tf_op jit(solution)/shard_map/ppermute | solution.py:18
  256.0 8.0 %collective-permute-start.22 = (bf16[64,18,1]{2,0,1:T(8,128)(2,1)S(1)}, bf16[64,18,1]{2,0,1:T(8,128)(2,1)S(1)}, u32[]{:S(2)}, u32[]{:S(2)}) collective-permute-start(bf16[64,18,1]{2,0,1:T(8,128)(2,1)S(1)} %get-tuple-element.64), channel_id=1, source_target_pairs={{1,0},{2,1},{3,2},{0,3},{5,4},{6,5},{7,6},{4,7},{9,8},{10,9},{11,1... | collective-permute-start | bytes 6920 | tf_op jit(solution)/shard_map/ppermute | solution.py:19
  278.6 6.6 %collective-permute-start.24 = (bf16[64,1,384]{2,0,1:T(8,128)(2,1)S(1)}, bf16[64,1,384]{2,0,1:T(8,128)(2,1)S(1)}, u32[]{:S(2)}, u32[]{:S(2)}) collective-permute-start(bf16[64,1,384]{2,0,1:T(8,128)(2,1)S(1)} %get-tuple-element.68), channel_id=1, source_target_pairs={{0,4},{4,8},{8,12},{12,16},{16,20},{20,24},{24,28},{28,0},{1,5},{5... | collective-permute-start | bytes 147464 | tf_op jit(solution)/shard_map/ppermute | solution.py:18
  281.3 4.2 collective-permute-start.25
  285.6 6.6 %collective-permute-start.27 = (bf16[64,18,1]{2,0,1:T(8,128)(2,1)S(1)}, bf16[64,18,1]{2,0,1:T(8,128)(2,1)S(1)}, u32[]{:S(2)}, u32[]{:S(2)}) collective-permute-start(bf16[64,18,1]{2,0,1:T(8,128)(2,1)S(1)} %get-tuple-element.59), channel_id=1, source_target_pairs={{0,1},{1,2},{2,3},{3,0},{4,5},{5,6},{6,7},{7,4},{8,9},{9,10},{10,1... | collective-permute-start | bytes 6920 | tf_op jit(solution)/shard_map/ppermute | solution.py:18
  286.0 8.9 %collective-permute-start.26 = (bf16[64,18,1]{2,0,1:T(8,128)(2,1)S(1)}, bf16[64,18,1]{2,0,1:T(8,128)(2,1)S(1)}, u32[]{:S(2)}, u32[]{:S(2)}) collective-permute-start(bf16[64,18,1]{2,0,1:T(8,128)(2,1)S(1)} %get-tuple-element.60), channel_id=1, source_target_pairs={{1,0},{2,1},{3,2},{0,3},{5,4},{6,5},{7,6},{4,7},{9,8},{10,9},{11,1... | collective-permute-start | bytes 6920 | tf_op jit(solution)/shard_map/ppermute | solution.py:19
  (17 other events, 598.5 us)
Sparse Core Ops, SparseCore 0:
  284.3 130.0 all-reduce.6
where the time goes:
time: 424 us; the launch traced here: 423 us
  blocking collectives  210 us (50%)
  waiting for transfers between devices  98.9 us (23%)
  starting transfers between devices  32.2 us (8%)
  between operations  28.6 us (7%)
  matrix products  23.7 us (6%)
  other arithmetic  15.2 us (4%)
  local copies, waits for them, and re-layouts  14.1 us (3%)
    psum x4, blocking collectives, paired_sums(): lax.psum((jnp.sum(residual * residual), jnp.sum(residual * image)), ('gx'...  167 us
    psum x1, waiting for transfers between devices, per_device(): lax.psum((grad_first, grad_middle, grad_last, bias_one, bias_two), ('gx',...  61.8 us
    psum x1, blocking collectives, per_device(): lax.psum((grad_first, grad_middle, grad_last, bias_one, bias_two), ('gx',...  43.5 us
    ppermute x14, waiting for transfers between devices, with_halo(): before = lax.ppermute(last, axis, up)  24.5 us
    ppermute x14, starting transfers between devices, with_halo(): before = lax.ppermute(last, axis, up)  17.7 us
    ppermute x14, starting transfers between devices, with_halo(): after = lax.ppermute(leading, axis, down)  14.4 us
    dot_general x27, matrix products, grads_from_padded_deltas(): lax.dot_general(shifted, flat_inputs, (((1,), (1,)), ((), ())), preferred...  14.4 us
    ppermute x14, waiting for transfers between devices, with_halo(): after = lax.ppermute(leading, axis, down)  12.6 us
  transfers between devices with their start and end apart: 29, of which 24 were waited for; matrix products, arithmetic and copies ran while one was open for 5% of the time, Pallas kernels for 0%

commit v1 on v0

--- a/solution.py
+++ b/solution.py
@@ -117,7 +117,9 @@
     grad_velocity = adjoint_pad[:, 1:-1, 1:-1] + spread
     bias_one = jnp.sum(delta1.astype(jnp.float32), axis=(1, 2))
     bias_two = jnp.sum(delta2.astype(jnp.float32), axis=(1, 2))
-    summed = lax.psum((grad_first, grad_middle, grad_last, bias_one, bias_two), ("gx", "gy"))
+    summed = lax.psum(
+        lax.psum((grad_first, grad_middle, grad_last, bias_one, bias_two), "gy"), "gx"
+    )
     return (
         grad_velocity,
         factor * summed[0],

time: 424 us -> 441 us (1.040)
  waiting for transfers between devices: 98.9 us -> 107 us
  blocking collectives: 210 us -> 217 us
    psum x1 -> x2, waiting for transfers between devices: 61.8 us -> 68.8 us  [the longest x1 68.8 us: per_device(): lax.psum(lax.psum((grad_first, grad_middle, grad_last, bias_one, bias_two...]
    psum x1 -> x2, blocking collectives: 43.5 us -> 50 us  [the longest x1 37.1 us: per_device(): lax.psum(lax.psum((grad_first, grad_middle, grad_last, bias_one, bias_two...]
  transfers between devices with their start and end apart: 29 -> 30, of which waited for: 24 -> 24; matrix products, arithmetic and copies ran while one was open for 5% -> 4% of each run, Pallas kernels for 0% -> 0%
where the time goes in v1:
time: 441 us; the launch traced here: 437 us
  blocking collectives  217 us (49%)
  waiting for transfers between devices  107 us (24%)
  starting transfers between devices  32.2 us (7%)
  between operations  28.6 us (6%)
  matrix products  23.7 us (5%)
  other arithmetic  15.2 us (3%)
  local copies, waits for them, and re-layouts  14.1 us (3%)
    psum x4, blocking collectives, paired_sums(): lax.psum((jnp.sum(residual * residual), jnp.sum(residual * image)), ('gx'...  167 us
    psum x1, waiting for transfers between devices, per_device(): lax.psum(lax.psum((grad_first, grad_middle, grad_last, bias_one, bias_two...  68.8 us
    psum x1, blocking collectives, per_device(): lax.psum(lax.psum((grad_first, grad_middle, grad_last, bias_one, bias_two...  37.1 us
    ppermute x14, waiting for transfers between devices, with_halo(): before = lax.ppermute(last, axis, up)  24.5 us
    ppermute x14, starting transfers between devices, with_halo(): before = lax.ppermute(last, axis, up)  17.8 us
    dot_general x27, matrix products, grads_from_padded_deltas(): lax.dot_general(shifted, flat_inputs, (((1,), (1,)), ((), ())), preferred...  14.4 us
    ppermute x14, starting transfers between devices, with_halo(): after = lax.ppermute(leading, axis, down)  14.4 us
    ppermute x14, waiting for transfers between devices, with_halo(): after = lax.ppermute(leading, axis, down)  13.3 us
  transfers between devices with their start and end apart: 30, of which 24 were waited for; matrix products, arithmetic and copies ran while one was open for 4% of the time, Pallas kernels for 0%

profile of v1, /device:TPU:8, one launch (start us, length us, event | category | flops | bytes accessed | tf_op | source)
XLA Modules:
  0.0 437.2 jit_solution(4897420195304831478)
XLA Ops:
  15.5 2.0 collective-permute-done.2
  18.5 2.5 collective-permute-start.4
  24.6 1.7 collective-permute-start.7
  28.4 42.3 %all-reduce.3 = (f32[]{:T(128)}, f32[]{:T(128)}) all-reduce(f32[]{:T(128)} %get-tuple-element.25, f32[]{:T(128)} %get-tuple-element.24), channel_id=1, replica_groups=mesh['gx'=8,'gy'=4] {'gx','gy'}, use_global_device_ids=true, to_apply=%region_1.0 | all-reduce | flops 2 | bytes 16 | tf_op jit(solution)/shard_map/psum | solution.py:46
  72.1 2.5 collective-permute-start.8
  78.3 1.7 collective-permute-start.11
  82.1 41.4 %all-reduce.2 = (f32[]{:T(128)}, f32[]{:T(128)}) all-reduce(f32[]{:T(128)} %get-tuple-element.23, f32[]{:T(128)} %get-tuple-element.22), channel_id=1, replica_groups=mesh['gx'=8,'gy'=4] {'gx','gy'}, use_global_device_ids=true, to_apply=%region_5.0 | all-reduce | flops 2 | bytes 16 | tf_op jit(solution)/shard_map/psum | solution.py:46
  128.3 2.5 collective-permute-start.12
  134.4 1.7 collective-permute-start.15
  138.3 41.7 %all-reduce.1 = (f32[]{:T(128)}, f32[]{:T(128)}) all-reduce(f32[]{:T(128)} %get-tuple-element.21, f32[]{:T(128)} %get-tuple-element.20), channel_id=1, replica_groups=mesh['gx'=8,'gy'=4] {'gx','gy'}, use_global_device_ids=true, to_apply=%region_9.0 | all-reduce | flops 2 | bytes 16 | tf_op jit(solution)/shard_map/psum | solution.py:46
  184.1 2.5 collective-permute-start.16
  190.3 1.7 collective-permute-start.19
  194.1 41.4 %all-reduce = (f32[]{:T(128)}, f32[]{:T(128)}) all-reduce(f32[]{:T(128)} %get-tuple-element.19, f32[]{:T(128)} %get-tuple-element.18), channel_id=1, replica_groups=mesh['gx'=8,'gy'=4] {'gx','gy'}, use_global_device_ids=true, to_apply=%region_13.0 | all-reduce | flops 2 | bytes 16 | tf_op jit(solution)/shard_map/psum | solution.py:46
  249.2 2.5 collective-permute-start.20
  252.6 1.6 collective-permute-done.20
  256.0 1.7 collective-permute-start.22
  258.1 5.7 %collective-permute-done.23 = bf16[64,18,1]{2,0,1:T(8,128)(2,1)S(1)} collective-permute-done((bf16[64,18,1]{2,0,1:T(8,128)(2,1)S(1)}, bf16[64,18,1]{2,0,1:T(8,128)(2,1)S(1)}, u32[]{:S(2)}, u32[]{:S(2)}) %collective-permute-start.23) | collective-permute-done | bytes 2336 | tf_op jit(solution)/shard_map/ppermute | solution.py:18
  278.6 2.7 collective-permute-start.24
  289.5 2.7 collective-permute-done.27
  292.2 3.4 collective-permute-done.26
  302.0 12.8 %all-reduce.5 = (f32[9,64,2]{1,2,0:T(2,128)S(1)}, f32[9,2,64]{2,1,0:T(2,128)S(1)}, f32[64]{0:T(128)S(1)}, f32[64]{0:T(128)S(1)}) all-reduce(f32[9,64,2]{1,2,0:T(2,128)S(1)} %fusion.40, f32[9,2,64]{2,1,0:T(2,128)S(1)} %fusion.31, f32[64]{0:T(128)S(1)} %get-tuple-element.44, ...), channel_id=1, replica_groups=mesh['gx'=8,'gy'=4] {'gy'}, use_global_device_ids=true, to_apply=%region_16.0 | all-reduce | flops 2432 | bytes 19456 | tf_op jit(solution)/shard_map/psum | solution.py:121
  314.8 37.1 %all-reduce.4 = (f32[9,64,2]{1,2,0:T(2,128)S(1)}, f32[9,2,64]{2,1,0:T(2,128)S(1)}, f32[64]{0:T(128)S(1)}, f32[64]{0:T(128)S(1)}) all-reduce(f32[9,64,2]{1,2,0:T(2,128)S(1)} %get-tuple-element.38, f32[9,2,64]{2,1,0:T(2,128)S(1)} %get-tuple-element.39, f32[64]{0:T(128)S(1)} %get-tuple-element.40, ...), channel_id=1, replica_groups=mesh['gx'=8,'gy'=4] {'gx'}, use_global_device_ids=true, to_apply=%region_17.0 | all-reduce | flops 2432 | bytes 19456 | tf_op jit(solution)/shard_map/psum | solution.py:120
  359.9 68.8 %all-reduce.11.cloned.1.call-done = f32[9,64,64]{2,1,0:T(8,128)} async-done(((f32[9,64,64]{2,1,0:T(8,128)}), f32[9,64,64]{2,1,0:T(8,128)}) %all-reduce.11.cloned.1.call-update) | async-done | bytes 147472 | tf_op jit(solution)/shard_map/psum | solution.py:120
  428.7 1.7 broadcast_multiply_fusion
  (185 shorter events, 81.9 us)
Async XLA Ops:
  7.2 352.1 %all-reduce.9.cloned.1.call-start = ((), (), s32[]{:S(2)}) async-start(), calls=%async_computation | async-start | bytes 589824 | tf_op jit(solution)/shard_map/psum | solution.py:121
  8.0 4.5 %collective-permute-start = (f32[2,1,384]{2,1,0:T(1,128)S(1)}, f32[2,1,384]{2,1,0:T(1,128)S(1)}, u32[]{:S(2)}, u32[]{:S(2)}) collective-permute-start(f32[2,1,384]{2,1,0:T(1,128)S(1)} %get-tuple-element.82), channel_id=1, source_target_pairs={{0,4},{4,8},{8,12},{12,16},{16,20},{20,24},{24,28},{28,0},{1,5},{5... | collective-permute-start | bytes 9224 | tf_op jit(solution)/shard_map/ppermute | solution.py:18
  9.5 3.6 collective-permute-start.1
  14.0 3.5 collective-permute-start.2
  18.5 4.5 %collective-permute-start.4 = (f32[2,384]{1,0:T(2,128)S(1)}, f32[2,384]{1,0:T(2,128)S(1)}, u32[]{:S(2)}, u32[]{:S(2)}) collective-permute-start(f32[2,384]{1,0:T(2,128)S(1)} %get-tuple-element.107), channel_id=1, source_target_pairs={{0,4},{4,8},{8,12},{12,16},{16,20},{20,24},{24,28},{28,0},{1,5},{5... | collective-permute-start | bytes 9224 | tf_op jit(solution)/shard_map/ppermute | solution.py:18
  20.9 3.6 collective-permute-start.5
  24.6 3.1 collective-permute-start.7
  72.1 4.5 %collective-permute-start.8 = (f32[2,384]{1,0:T(2,128)S(1)}, f32[2,384]{1,0:T(2,128)S(1)}, u32[]{:S(2)}, u32[]{:S(2)}) collective-permute-start(f32[2,384]{1,0:T(2,128)S(1)} %get-tuple-element.105), channel_id=1, source_target_pairs={{0,4},{4,8},{8,12},{12,16},{16,20},{20,24},{24,28},{28,0},{1,5},{5... | collective-permute-start | bytes 9224 | tf_op jit(solution)/shard_map/ppermute | solution.py:18
  74.6 3.6 collective-permute-start.9
  78.3 3.1 collective-permute-start.11
  128.3 4.5 %collective-permute-start.12 = (f32[2,384]{1,0:T(2,128)S(1)}, f32[2,384]{1,0:T(2,128)S(1)}, u32[]{:S(2)}, u32[]{:S(2)}) collective-permute-start(f32[2,384]{1,0:T(2,128)S(1)} %get-tuple-element.103), channel_id=1, source_target_pairs={{0,4},{4,8},{8,12},{12,16},{16,20},{20,24},{24,28},{28,0},{1,5},{5... | collective-permute-start | bytes 9224 | tf_op jit(solution)/shard_map/ppermute | solution.py:18
  130.8 3.6 collective-permute-start.13
  184.1 4.5 %collective-permute-start.16 = (f32[2,384]{1,0:T(2,128)S(1)}, f32[2,384]{1,0:T(2,128)S(1)}, u32[]{:S(2)}, u32[]{:S(2)}) collective-permute-start(f32[2,384]{1,0:T(2,128)S(1)} %get-tuple-element.101), channel_id=1, source_target_pairs={{0,4},{4,8},{8,12},{12,16},{16,20},{20,24},{24,28},{28,0},{1,5},{5... | collective-permute-start | bytes 9224 | tf_op jit(solution)/shard_map/ppermute | solution.py:18
  186.6 3.6 collective-permute-start.17
  190.3 3.1 collective-permute-start.19
  249.2 5.0 %collective-permute-start.20 = (bf16[64,1,384]{2,0,1:T(8,128)(2,1)S(1)}, bf16[64,1,384]{2,0,1:T(8,128)(2,1)S(1)}, u32[]{:S(2)}, u32[]{:S(2)}) collective-permute-start(bf16[64,1,384]{2,0,1:T(8,128)(2,1)S(1)} %get-tuple-element.76), channel_id=1, source_target_pairs={{0,4},{4,8},{8,12},{12,16},{16,20},{20,24},{24,28},{28,0},{1,5},{5... | collective-permute-start | bytes 147464 | tf_op jit(solution)/shard_map/ppermute | solution.py:18
  251.7 4.1 collective-permute-start.21
  256.0 7.8 %collective-permute-start.23 = (bf16[64,18,1]{2,0,1:T(8,128)(2,1)S(1)}, bf16[64,18,1]{2,0,1:T(8,128)(2,1)S(1)}, u32[]{:S(2)}, u32[]{:S(2)}) collective-permute-start(bf16[64,18,1]{2,0,1:T(8,128)(2,1)S(1)} %get-tuple-element.67), channel_id=1, source_target_pairs={{0,1},{1,2},{2,3},{3,0},{4,5},{5,6},{6,7},{7,4},{8,9},{9,10},{10,1... | collective-permute-start | bytes 6920 | tf_op jit(solution)/shard_map/ppermute | solution.py:18
  256.0 8.0 %collective-permute-start.22 = (bf16[64,18,1]{2,0,1:T(8,128)(2,1)S(1)}, bf16[64,18,1]{2,0,1:T(8,128)(2,1)S(1)}, u32[]{:S(2)}, u32[]{:S(2)}) collective-permute-start(bf16[64,18,1]{2,0,1:T(8,128)(2,1)S(1)} %get-tuple-element.68), channel_id=1, source_target_pairs={{1,0},{2,1},{3,2},{0,3},{5,4},{6,5},{7,6},{4,7},{9,8},{10,9},{11,1... | collective-permute-start | bytes 6920 | tf_op jit(solution)/shard_map/ppermute | solution.py:19
  278.6 6.7 %collective-permute-start.24 = (bf16[64,1,384]{2,0,1:T(8,128)(2,1)S(1)}, bf16[64,1,384]{2,0,1:T(8,128)(2,1)S(1)}, u32[]{:S(2)}, u32[]{:S(2)}) collective-permute-start(bf16[64,1,384]{2,0,1:T(8,128)(2,1)S(1)} %get-tuple-element.72), channel_id=1, source_target_pairs={{0,4},{4,8},{8,12},{12,16},{16,20},{20,24},{24,28},{28,0},{1,5},{5... | collective-permute-start | bytes 147464 | tf_op jit(solution)/shard_map/ppermute | solution.py:18
  281.3 4.2 collective-permute-start.25
  284.2 144.5 %all-reduce.11.cloned.1.call-start = ((), (), s32[]{:S(2)}) async-start(), calls=%async_computation.1 | async-start | bytes 589824 | tf_op jit(solution)/shard_map/psum | solution.py:120
  285.6 6.6 %collective-permute-start.27 = (bf16[64,18,1]{2,0,1:T(8,128)(2,1)S(1)}, bf16[64,18,1]{2,0,1:T(8,128)(2,1)S(1)}, u32[]{:S(2)}, u32[]{:S(2)}) collective-permute-start(bf16[64,18,1]{2,0,1:T(8,128)(2,1)S(1)} %get-tuple-element.63), channel_id=1, source_target_pairs={{0,1},{1,2},{2,3},{3,0},{4,5},{5,6},{6,7},{7,4},{8,9},{9,10},{10,1... | collective-permute-start | bytes 6920 | tf_op jit(solution)/shard_map/ppermute | solution.py:18
  286.1 9.6 %collective-permute-start.26 = (bf16[64,18,1]{2,0,1:T(8,128)(2,1)S(1)}, bf16[64,18,1]{2,0,1:T(8,128)(2,1)S(1)}, u32[]{:S(2)}, u32[]{:S(2)}) collective-permute-start(bf16[64,18,1]{2,0,1:T(8,128)(2,1)S(1)} %get-tuple-element.64), channel_id=1, source_target_pairs={{1,0},{2,1},{3,2},{0,3},{5,4},{6,5},{7,6},{4,7},{9,8},{10,9},{11,1... | collective-permute-start | bytes 6920 | tf_op jit(solution)/shard_map/ppermute | solution.py:19
  (18 other events, 608.3 us)
Sparse Core Ops, SparseCore 0:
  284.3 35.1 all-reduce.8
  359.5 69.1 all-reduce.10
